TPU v7x, 32 devices: a whole 2x2x4 slice. The times are simulated.
32 devices in a mesh: cache: 8 (over z, x), owner: 4 (over y, core).
Axes of the slice: x: 2, y: 2, z: 4, core: 2. Of those that a mesh axis runs over, the one named last changes fastest.
Arguments:
- cache: bfloat16 [32, 4, 128, 256], P('cache'), may hold values from -2.5 to 2.5
- backing: bfloat16 [32, 32, 128, 256], P('cache', 'owner'), may hold values from -2.5 to 2.5
- resident: int32 [32, 4], P('cache'), may hold values from 0 to 31, as said below
- promote: int32 [32, 2], P('cache'), may hold values from 0 to 31, as said below
- victim: int32 [32, 2], P('cache'), may hold values from 0 to 3, as said below
- lookups: int32 [2, 4096, 32, 8], P(None, 'owner', 'cache'), may hold values from 0 to 511
- route: int32 [2, 4, 1024], P(None, 'owner'), may hold values from 0 to 1023, each once within a row
- dcn_down: bfloat16 [8192, 128], P('cache'), may hold values from -0.0625 to 0.0625
- dcn_up: bfloat16 [128, 8192], P(None, 'cache'), may hold values from -0.5 to 0.5
- dcn_bias: float32 [8192], replicated, may hold values from -5 to 5
- mlp_in: bfloat16 [8192, 1024], P('cache'), may hold values from -0.0625 to 0.0625
- mlp_bias: float32 [1024], replicated, may hold values from -3 to 3
- mlp_out: float32 [1024], replicated, may hold values from -0.1875 to 0.1875
- out_bias: float32 [1], replicated, may hold values from -4 to 4
Outputs:
- scores: float32 [2, 4, 1024], P(None, 'owner', 'cache')
- new_cache: bfloat16 [32, 4, 128, 256], P('cache')
- new_backing: bfloat16 [32, 32, 128, 256], P('cache', 'owner')
Inputs may be any that keep to these rules, and one draw needn't show every extreme that they name: `resident`: for each feature, 4 distinct backing blocks. `promote`: for each feature, 2 distinct backing blocks, none of them in that feature's resident; block k belongs to owner k // 8. `victim`: for each feature, 2 distinct slots. `route`: each batch and owner group holds every request index once.
All inputs are finite; a program needn't handle non-finite values.
Results may differ from a plain program's by a relative error of at most 0.004.
Values may be sent and summed in bfloat16 or wider, within the bound.
A program may use at most 128 MiB of HBM per device.

v0:
```python
import jax
import jax.numpy as jnp
from jax import lax
from jax.sharding import PartitionSpec as P


def take_rows(table, wanted):
    return jax.vmap(lambda rows, chosen: rows[chosen])(table, wanted)


def pool_batch(requests, order, table):
    requests = requests[order]
    count = requests.shape[0]
    step = min(512, count)
    codes = jnp.arange(table.shape[1], dtype=jnp.int32)

    def one_block(lookup_block):
        counts = jnp.sum((lookup_block[..., None] == codes).astype(jnp.bfloat16), axis=2)
        return jnp.einsum("rfk,fke->rfe", counts, table, preferred_element_type=jnp.float32).astype(
            jnp.bfloat16
        )

    blocks = requests.reshape((count // step, step) + requests.shape[1:])
    pooled = lax.map(one_block, blocks)
    return pooled.reshape((count,) + pooled.shape[2:])


def on_device(
    cache,
    backing,
    resident,
    promote,
    victim,
    lookups,
    route,
    dcn_down,
    dcn_up,
    dcn_bias,
    mlp_in,
    mlp_bias,
    mlp_out,
    out_bias,
):
    held = cache.shape[0]
    slots = cache.shape[1]
    block = cache.shape[2]
    width = cache.shape[3]
    own_blocks = backing.shape[1]
    promoted_count = promote.shape[1]
    owner_here = lax.axis_index("owner")
    local_index = promote - owner_here * own_blocks
    owned_here = (local_index >= 0) & (local_index < own_blocks)
    clamped = jnp.clip(local_index, 0, own_blocks - 1)
    fetched = take_rows(backing, clamped)
    outgoing = jnp.where(owned_here[:, :, None, None], fetched, jnp.zeros_like(fetched))
    arrived = lax.all_gather(outgoing, "owner", axis=0, tiled=True)
    owners = arrived.shape[0] // held
    arrived = arrived.reshape(owners, held, promoted_count, block, width)
    source = promote // own_blocks
    picked = source[None] == jnp.arange(owners, dtype=jnp.int32)[:, None, None]
    promoted = jnp.sum(jnp.where(picked[..., None, None], arrived, jnp.zeros_like(arrived)), axis=0)
    evicted = take_rows(cache, victim)
    leaving = take_rows(resident, victim) - owner_here * own_blocks
    slot_numbers = jnp.arange(slots, dtype=jnp.int32)
    block_numbers = jnp.arange(own_blocks, dtype=jnp.int32)
    new_cache = cache
    new_backing = backing
    for column in range(promoted_count):
        slot_hit = victim[:, column][:, None] == slot_numbers[None, :]
        new_cache = jnp.where(slot_hit[:, :, None, None], promoted[:, column][:, None], new_cache)
        block_hit = leaving[:, column][:, None] == block_numbers[None, :]
        new_backing = jnp.where(
            block_hit[:, :, None, None], evicted[:, column][:, None], new_backing
        )
    table = new_cache.reshape(held, slots * block, width)
    batches = lookups.shape[0]
    received = []
    for batch_turn in range(batches):
        pooled = pool_batch(lookups[batch_turn], route[batch_turn, 0], table)
        received.append(lax.all_to_all(pooled, "cache", split_axis=0, concat_axis=1, tiled=True))
    arrived_rows = jnp.stack(received)
    per_batch = arrived_rows.shape[1]
    features = arrived_rows.reshape(batches * per_batch, -1)
    low = jnp.dot(
        features,
        lax.all_gather(dcn_down, "cache", axis=0, tiled=True),
        preferred_element_type=jnp.float32,
    ).astype(jnp.bfloat16)
    gate = (
        jnp.dot(
            low,
            lax.all_gather(dcn_up, "cache", axis=1, tiled=True),
            preferred_element_type=jnp.float32,
        )
        + dcn_bias
    )
    crossed = (features * gate + features).astype(jnp.bfloat16)
    portion = mlp_in.shape[1] // lax.axis_size("owner")
    own_columns = lax.dynamic_slice_in_dim(mlp_in, owner_here * portion, portion, 1)
    column_block = lax.all_gather(own_columns, "cache", axis=0, tiled=True)
    before = jnp.dot(
        crossed,
        lax.all_gather(column_block, "owner", axis=1, tiled=True),
        preferred_element_type=jnp.float32,
    )
    hidden = jnp.maximum(before + mlp_bias, 0.0)
    scores = jnp.sum(hidden * mlp_out, axis=-1) + out_bias[0]
    return (scores.reshape(batches, 1, per_batch), new_cache, new_backing)


def solution(mesh):
    in_specs = (
        P("cache", None, None, None),
        P("cache", "owner", None, None),
        P("cache", None),
        P("cache", None),
        P("cache", None),
        P(None, "owner", "cache", None),
        P(None, "owner", None),
        P("cache", None),
        P(None, "cache"),
        P(),
        P("cache", None),
        P(),
        P(),
        P(),
    )
    out_specs = (
        P(None, "owner", "cache"),
        P("cache", None, None, None),
        P("cache", "owner", None, None),
    )
    return jax.shard_map(
        on_device, mesh=mesh, in_specs=in_specs, out_specs=out_specs, check_vma=False
    )
```

profile of v0, /device:TPU:0, one launch (start us, length us, event | category | flops | bytes accessed | tf_op | source)
XLA Modules:
  0.0 392.6 jit_solution(9065323531690684591)
XLA Ops:
  11.4 2.2 gather_fusion.2
  15.8 70.4 %all-gather.12.cloned.1.call-done = bf16[8192,256]{1,0:T(8,128)(2,1)} async-done(((bf16[1024,256]{1,0:T(8,128)(2,1)}), bf16[8192,256]{1,0:T(8,128)(2,1)}) %all-gather.12.cloned.1.call-update) | async-done | bytes 4194320 | tf_op jit(solution)/shard_map/all_gather | solution.py:100
  88.1 7.9 %gather_fusion = s32[1024,4,8]{2,1,0:T(4,128)} fusion(s32[1024,4,8]{2,1,0:T(4,128)S(1)} %bitcast.100, s32[1024]{0:T(1024)S(1)} %broadcast_clamp_fusion.1), kind=kCustom, calls=%fused_computation | custom fusion | bytes 266240 | tf_op jit(solution)/shard_map/gather | solution.py:12
  96.0 1.8 copy.113
  98.0 10.9 %all-gather.6.cloned.1.call-done = bf16[16,2,128,256]{3,2,1,0:T(8,128)(2,1)} async-done(((bf16[4,2,128,256]{3,2,1,0:T(8,128)(2,1)}), bf16[16,2,128,256]{3,2,1,0:T(8,128)(2,1)}) %all-gather.6.cloned.1.call-update) | async-done | bytes 2097168 | tf_op jit(solution)/shard_map/all_gather | solution.py:56
  108.9 2.1 select_reduce_fusion
  113.7 27.7 %while.26 = (s32[]{:T(128)}, bf16[2,512,4,256]{3,1,0,2:T(8,128)(2,1)}, s32[2,512,4,8]{1,3,2,0:T(8,128)S(1)}, bf16[4,512,256]{2,1,0:T(8,128)(2,1)}, s32[]{:T(128)}) while((s32[]{:T(128)}, bf16[2,512,4,256]{3,1,0,2:T(8,128)(2,1)}, s32[2,512,4,8]{1,3,2,0:T(8,128)S(1)}, bf16[4,512,256]{2,1,0:T(8,128)(2,1)}, s32[]{:T(128)}) %tuple.91), condition=%wide.region_3.4_spmd.clone, body=%wide.region_1.3_spmd.clone.sunk | while | flops 561512448 | bytes 10814045 | solution.py:24
  114.2 11.7 %fusion.60 = bf16[512,4,512]{2,1,0:T(4,128)(2,1)S(1)} fusion(s32[512,4,8]{2,1,0:T(4,128)S(1)} %copy.164), kind=kLoop, calls=%fused_computation.9.clone.1 | loop fusion | flops 24117248 | bytes 2162688 | tf_op jit(solution)/shard_map/while/body/eval_jaxpr/reduce_sum | solution.py:18
  125.9 1.7 fusion.61
  128.0 11.7 %fusion.60 = bf16[512,4,512]{2,1,0:T(4,128)(2,1)S(1)} fusion(s32[512,4,8]{2,1,0:T(4,128)S(1)} %copy.164), kind=kLoop, calls=%fused_computation.9.clone.1 | loop fusion | flops 24117248 | bytes 2162688 | tf_op jit(solution)/shard_map/while/body/eval_jaxpr/reduce_sum | solution.py:18
  139.8 1.7 fusion.61
  141.5 4.5 %copy.115 = bf16[1024,4,256]{2,1,0:T(4,128)(2,1)} copy(bf16[1024,4,256]{2,0,1:T(8,128)(2,1)} %bitcast.12) | data formatting | bytes 4194304 | tf_op jit(solution)/shard_map/reshape | solution.py:25
  146.0 5.5 %all-to-all-start = ((bf16[1024,4,256]{2,1,0:T(4,128)(2,1)}), bf16[1024,4,256]{2,1,0:T(4,128)(2,1)}, u32[]{:S(2)}, u32[]{:S(2)}) async-start(bf16[1024,4,256]{2,1,0:T(4,128)(2,1)} %copy.115), calls=%async_computation | async-start | bytes 4194304 | tf_op jit(solution)/shard_map/all_to_all | solution.py:80
  152.3 7.9 %gather_fusion.1 = s32[1024,4,8]{2,1,0:T(4,128)} fusion(s32[1024,4,8]{2,1,0:T(4,128)S(1)} %bitcast.101, s32[1024]{0:T(1024)S(1)} %broadcast_clamp_fusion), kind=kCustom, calls=%fused_computation.1 | custom fusion | bytes 266240 | tf_op jit(solution)/shard_map/gather | solution.py:12
  160.3 1.8 copy.120
  163.6 27.7 %while.27 = (s32[]{:T(128)}, bf16[2,512,4,256]{3,1,0,2:T(8,128)(2,1)}, s32[2,512,4,8]{1,3,2,0:T(8,128)S(1)}, bf16[4,512,256]{2,1,0:T(8,128)(2,1)}, s32[]{:T(128)}) while((s32[]{:T(128)}, bf16[2,512,4,256]{3,1,0,2:T(8,128)(2,1)}, s32[2,512,4,8]{1,3,2,0:T(8,128)S(1)}, bf16[4,512,256]{2,1,0:T(8,128)(2,1)}, s32[]{:T(128)}) %tuple.92), condition=%wide.region_6.7_spmd.clone, body=%wide.region_4.6_spmd.clone.sunk | while | flops 561512448 | bytes 10814045 | solution.py:24
  164.0 11.7 %fusion.64 = bf16[512,4,512]{2,1,0:T(4,128)(2,1)S(1)} fusion(s32[512,4,8]{2,1,0:T(4,128)S(1)} %copy.166), kind=kLoop, calls=%fused_computation.18.clone.1 | loop fusion | flops 24117248 | bytes 2162688 | tf_op jit(solution)/shard_map/while/body/eval_jaxpr/reduce_sum | solution.py:18
  175.7 1.7 fusion.65
  177.8 11.7 %fusion.64 = bf16[512,4,512]{2,1,0:T(4,128)(2,1)S(1)} fusion(s32[512,4,8]{2,1,0:T(4,128)S(1)} %copy.166), kind=kLoop, calls=%fused_computation.18.clone.1 | loop fusion | flops 24117248 | bytes 2162688 | tf_op jit(solution)/shard_map/while/body/eval_jaxpr/reduce_sum | solution.py:18
  189.6 1.7 fusion.65
  191.3 4.6 %copy.122 = bf16[1024,4,256]{2,1,0:T(4,128)(2,1)} copy(bf16[1024,4,256]{2,0,1:T(8,128)(2,1)} %bitcast.20) | data formatting | bytes 4194304 | tf_op jit(solution)/shard_map/reshape | solution.py:25
  195.9 17.7 %all-to-all-done = bf16[1024,4,256]{2,1,0:T(4,128)(2,1)} async-done(((bf16[1024,4,256]{2,1,0:T(4,128)(2,1)}), bf16[1024,4,256]{2,1,0:T(4,128)(2,1)}, u32[]{:S(2)}, u32[]{:S(2)}) %all-to-all-start) | async-done | bytes 2097184 | tf_op jit(solution)/shard_map/all_to_all | solution.py:80
  213.6 4.6 %all-to-all-start.1 = ((bf16[1024,4,256]{2,1,0:T(4,128)(2,1)}), bf16[1024,4,256]{2,1,0:T(4,128)(2,1)}, u32[]{:S(2)}, u32[]{:S(2)}) async-start(bf16[1024,4,256]{2,1,0:T(4,128)(2,1)} %copy.122), calls=%async_computation.1 | async-start | bytes 4194304 | tf_op jit(solution)/shard_map/all_to_all | solution.py:80
  220.7 3.3 select_select_fusion
  224.0 1.9 copy.116
  227.4 53.9 %all-to-all-done.1 = bf16[1024,4,256]{2,1,0:T(4,128)(2,1)} async-done(((bf16[1024,4,256]{2,1,0:T(4,128)(2,1)}), bf16[1024,4,256]{2,1,0:T(4,128)(2,1)}, u32[]{:S(2)}, u32[]{:S(2)}) %all-to-all-start.1) | async-done | bytes 2097184 | tf_op jit(solution)/shard_map/all_to_all | solution.py:80
  281.3 1.9 copy.123
  285.3 2.4 copy.125
  287.7 6.3 %copy.142 = bf16[32,8,32,256]{3,1,2,0:T(8,128)(2,1)} copy(bf16[32,8,32,256]{3,2,1,0:T(8,128)(2,1)S(1)} %bitcast.99) | data formatting | bytes 8388608
  294.0 4.3 %convolution_convert_fusion = bf16[256,128]{1,0:T(8,128)(2,1)S(1)} fusion(bf16[256,8192]{1,0:T(8,128)(2,1)} %bitcast.97, bf16[8192,128]{1,0:T(8,128)(2,1)} %all-gather.8.cloned.1.call-done), kind=kOutput, calls=%fused_computation.35 | convolution fusion | flops 536903680 | bytes 6356992 | tf_op jit(solution)/shard_map/dot_general | solution.py:84
  298.3 74.4 %all-gather.14.cloned.1.call-done = bf16[8192,1024]{1,0:T(8,128)(2,1)} async-done(((bf16[8192,256]{1,0:T(8,128)(2,1)}), bf16[8192,1024]{1,0:T(8,128)(2,1)}) %all-gather.14.cloned.1.call-update) | async-done | bytes 16777232 | tf_op jit(solution)/shard_map/all_gather | solution.py:103
  372.7 12.8 %fusion.33 = f32[256]{0:T(256)S(1)} fusion(bf16[8192,1024]{1,0:T(8,128)(2,1)} %all-gather.14.cloned.1.call-done, bf16[256,128]{1,0:T(8,128)(2,1)S(1)} %convolution_convert_fusion, bf16[128,8192]{1,0:T(8,128)(2,1)} %all-gather.10.cloned.1.call-done, bf16[256,8192]{1,0:T(8,128)(2,1)} %bitcast.98, f32[8192]{0:T(1024)S(1)} %copy-done.12, ...), kind=kOutput, calls=%fused_computation.34 | convolution fusion | flops 4843372544 | bytes 23176192 | tf_op jit(solution)/shard_map/dot_general | solution.py:101
  (90 shorter events, 20.9 us)
Async XLA Ops:
  7.2 1.6 copy-start
  7.2 79.0 %all-gather.12.cloned.1.call-start = ((), (), s32[]{:S(2)}) async-start(), calls=%async_computation.5 | async-start | bytes 4718592 | tf_op jit(solution)/shard_map/all_gather | solution.py:100
  9.6 99.3 %all-gather.6.cloned.1.call-start = ((), (), s32[]{:S(2)}) async-start(), calls=%async_computation.2 | async-start | bytes 2621440 | tf_op jit(solution)/shard_map/all_gather | solution.py:56
  14.5 279.5 %all-gather.8.cloned.1.call-start = ((), (), s32[]{:S(2)}) async-start(), calls=%async_computation.3 | async-start | bytes 2359296 | tf_op jit(solution)/shard_map/all_gather | solution.py:86
  15.2 283.1 %all-gather.10.cloned.1.call-start = ((), (), s32[]{:S(2)}) async-start(), calls=%async_computation.4 | async-start | bytes 2359296 | tf_op jit(solution)/shard_map/all_gather | solution.py:92
  15.8 356.9 %all-gather.14.cloned.1.call-start = ((), (), s32[]{:S(2)}) async-start(), calls=%async_computation.6 | async-start | bytes 20971520 | tf_op jit(solution)/shard_map/all_gather | solution.py:103
  86.2 0.7 copy-start.9
  86.2 1.0 copy-start.8
  86.3 1.8 copy-start.10
  96.0 1.9 copy-start.11
  97.9 13.2 %copy-start.4 = (bf16[4,4,128,256]{3,2,1,0:T(8,128)(2,1)S(1)}, bf16[4,4,128,256]{3,2,1,0:T(8,128)(2,1)}, u32[]{:S(2)}) copy-start(bf16[4,4,128,256]{3,2,1,0:T(8,128)(2,1)} %param.18) | copy-start | bytes 3145732
  114.2 11.7 %copy-start.6 = (bf16[4,512,256]{2,1,0:T(8,128)(2,1)S(1)}, bf16[4,512,256]{2,1,0:T(8,128)(2,1)}, u32[]{:S(2)}) copy-start(bf16[4,512,256]{2,1,0:T(8,128)(2,1)} %get-tuple-element.305) | copy-start | bytes 3145732 | tf_op jit(solution)/shard_map/while
  128.0 11.7 %copy-start.6 = (bf16[4,512,256]{2,1,0:T(8,128)(2,1)S(1)}, bf16[4,512,256]{2,1,0:T(8,128)(2,1)}, u32[]{:S(2)}) copy-start(bf16[4,512,256]{2,1,0:T(8,128)(2,1)} %get-tuple-element.305) | copy-start | bytes 3145732 | tf_op jit(solution)/shard_map/while
  146.0 67.6 %all-to-all-start = ((bf16[1024,4,256]{2,1,0:T(4,128)(2,1)}), bf16[1024,4,256]{2,1,0:T(4,128)(2,1)}, u32[]{:S(2)}, u32[]{:S(2)}) async-start(bf16[1024,4,256]{2,1,0:T(4,128)(2,1)} %copy.115), calls=%async_computation | async-start | bytes 4194304 | tf_op jit(solution)/shard_map/all_to_all | solution.py:80
  164.0 11.7 %copy-start.7 = (bf16[4,512,256]{2,1,0:T(8,128)(2,1)S(1)}, bf16[4,512,256]{2,1,0:T(8,128)(2,1)}, u32[]{:S(2)}) copy-start(bf16[4,512,256]{2,1,0:T(8,128)(2,1)} %get-tuple-element.290) | copy-start | bytes 3145732 | tf_op jit(solution)/shard_map/while
  177.8 11.7 %copy-start.7 = (bf16[4,512,256]{2,1,0:T(8,128)(2,1)S(1)}, bf16[4,512,256]{2,1,0:T(8,128)(2,1)}, u32[]{:S(2)}) copy-start(bf16[4,512,256]{2,1,0:T(8,128)(2,1)} %get-tuple-element.290) | copy-start | bytes 3145732 | tf_op jit(solution)/shard_map/while
  195.9 23.1 %copy-start.5 = (bf16[4,4,128,256]{3,2,1,0:T(8,128)(2,1)S(1)}, bf16[4,4,128,256]{3,2,1,0:T(8,128)(2,1)}, u32[]{:S(2)}) copy-start(bf16[4,4,128,256]{3,2,1,0:T(8,128)(2,1)} %param.18) | copy-start | bytes 3145732
  195.9 23.7 %copy-start.2 = (s32[4,4]{1,0:T(4,128)S(1)}, s32[4,4]{1,0:T(4,128)}, u32[]{:S(2)}) copy-start(s32[4,4]{1,0:T(4,128)} %param.20) | copy-start | bytes 196
  213.6 67.7 %all-to-all-start.1 = ((bf16[1024,4,256]{2,1,0:T(4,128)(2,1)}), bf16[1024,4,256]{2,1,0:T(4,128)(2,1)}, u32[]{:S(2)}, u32[]{:S(2)}) async-start(bf16[1024,4,256]{2,1,0:T(4,128)(2,1)} %copy.122), calls=%async_computation.1 | async-start | bytes 4194304 | tf_op jit(solution)/shard_map/all_to_all | solution.py:80
  283.2 1.6 copy-start.3
  294.0 78.7 %copy-start.12 = (f32[8192]{0:T(1024)S(1)}, f32[8192]{0:T(1024)}, u32[]{:S(2)}) copy-start(f32[8192]{0:T(1024)} %param.27) | copy-start | bytes 98308
  294.0 78.7 %copy-start.13 = (f32[1024]{0:T(1024)S(1)}, f32[1024]{0:T(1024)}, u32[]{:S(2)}) copy-start(f32[1024]{0:T(1024)} %param.30) | copy-start | bytes 12292
  294.0 78.7 %copy-start.14 = (f32[1024]{0:T(1024)S(1)}, f32[1024]{0:T(1024)}, u32[]{:S(2)}) copy-start(f32[1024]{0:T(1024)} %param.29) | copy-start | bytes 12292
  372.7 13.4 %copy-start.1 = (bf16[1024,1024]{1,0:T(8,128)(2,1)S(1)}, bf16[1024,1024]{1,0:T(8,128)(2,1)}, u32[]{:S(2)}) copy-start(bf16[1024,1024]{1,0:T(8,128)(2,1)} %param.28) | copy-start | bytes 6291460
Sparse Core Ops, SparseCore 0:
  10.7 75.4 all-gather.11
  87.8 21.0 all-gather.5
  111.1 52.2 all-gather.7
  165.3 89.3 all-gather.9
  256.2 116.5 all-gather.13
where the time goes:
time: 393 us
  waiting for transfers between devices  229 us (58%)
  local copies, waits for them, and re-layouts  58.2 us (15%)
  other arithmetic  56.9 us (14%)
  matrix products  23.8 us (6%)
  between operations  14.7 us (4%)
  starting transfers between devices  10.3 us (3%)
    all_gather x1, waiting for transfers between devices, on_device(): lax.all_gather(column_block, 'owner', axis=1, tiled=True)  74.4 us
    all_to_all x2, waiting for transfers between devices, on_device(): lax.all_to_all(pooled, 'cache', split_axis=0, concat_axis=1, tiled=True)  71.6 us
    all_gather x1, waiting for transfers between devices, on_device(): column_block = lax.all_gather(own_columns, 'cache', axis=0, tiled=True)  70.4 us
    reduce_sum x4, other arithmetic, one_block(): jnp.sum((lookup_block[..., None] == codes).astype(jnp.bfloat16), axis=2)  46.9 us
    gather x2, local copies, waits for them, and re-layouts, pool_batch(): requests = requests[order]  15.8 us
    unnamed x31, local copies, waits for them, and re-layouts  15.5 us
    dot_general x1, matrix products, on_device(): jnp.dot(crossed, lax.all_gather(column_block, 'owner', axis=1, tiled=True...  12.8 us
    all_gather x1, waiting for transfers between devices, on_device(): arrived = lax.all_gather(outgoing, 'owner', axis=0, tiled=True)  10.9 us
  transfers between devices with their start and end apart: 7, of which 5 were waited for; matrix products, arithmetic and copies ran while one was open for 31% of the time, Pallas kernels for 0%

commit v1 on v0

v1 whole, which is shorter than its diff:
```python
import jax
import jax.numpy as jnp
from jax import lax
from jax.experimental import pallas as pl
from jax.experimental.pallas import tpu as pltpu
from jax.sharding import PartitionSpec as P


def take_rows(table, wanted):
    return jax.vmap(lambda rows, chosen: rows[chosen])(table, wanted)


def promote_blocks(cache, backing, resident, promote, victim):
    held, slots, block, width = cache.shape
    own_blocks = backing.shape[1]
    promoted_count = promote.shape[1]
    owner_here = lax.axis_index("owner")
    local_index = promote - owner_here * own_blocks
    owned_here = (local_index >= 0) & (local_index < own_blocks)
    clamped = jnp.clip(local_index, 0, own_blocks - 1)
    fetched = take_rows(backing, clamped)
    outgoing = jnp.where(owned_here[:, :, None, None], fetched, jnp.zeros_like(fetched))
    arrived = lax.all_gather(outgoing, "owner", axis=0, tiled=True)
    owners = arrived.shape[0] // held
    arrived = arrived.reshape(owners, held, promoted_count, block, width)
    source = promote // own_blocks
    picked = source[None] == jnp.arange(owners, dtype=jnp.int32)[:, None, None]
    promoted = jnp.sum(jnp.where(picked[..., None, None], arrived, jnp.zeros_like(arrived)), axis=0)
    evicted = take_rows(cache, victim)
    leaving = take_rows(resident, victim) - owner_here * own_blocks
    slot_numbers = jnp.arange(slots, dtype=jnp.int32)
    block_numbers = jnp.arange(own_blocks, dtype=jnp.int32)
    new_cache = cache
    new_backing = backing
    for column in range(promoted_count):
        slot_hit = victim[:, column][:, None] == slot_numbers[None, :]
        new_cache = jnp.where(slot_hit[:, :, None, None], promoted[:, column][:, None], new_cache)
        block_hit = leaving[:, column][:, None] == block_numbers[None, :]
        new_backing = jnp.where(
            block_hit[:, :, None, None], evicted[:, column][:, None], new_backing
        )
    return new_cache, new_backing


def routed(lookups, route):
    batches, count, held, bag = lookups.shape
    flat = lookups.reshape(batches, count, held * bag)
    halves = jnp.concatenate([flat // 256, flat % 256], axis=-1).astype(jnp.bfloat16)
    pick = (route[:, 0, :, None] == jnp.arange(count, dtype=jnp.int32)).astype(jnp.bfloat16)
    got = jnp.einsum("bpr,brj->bpj", pick, halves, preferred_element_type=jnp.float32)
    upper, lower = jnp.split(got, 2, axis=-1)
    return (upper * 256.0 + lower).reshape(batches * count, held * bag)


def pool_kernel(held, bag, codes_ref, table_ref, out_ref):
    rows_total, width = table_ref.shape[1], table_ref.shape[2]
    step = codes_ref.shape[0]
    lane = lax.broadcasted_iota(jnp.int32, (step, 128), 1).astype(jnp.float32)
    low_lane = lane.astype(jnp.bfloat16)
    high_lane = (lane + 128.0).astype(jnp.bfloat16)
    one = jnp.ones((step, 128), jnp.bfloat16)
    zero = jnp.zeros((step, 128), jnp.bfloat16)
    for f in range(held):
        parts = [zero] * (rows_total // 128)
        for l in range(bag):
            j = f * bag + l
            spread = jnp.broadcast_to(codes_ref[:, j : j + 1], (step, 128))
            for base in range(0, rows_total, 256):
                near = (spread - float(base)).astype(jnp.bfloat16)
                for half, numbers in enumerate((low_lane, high_lane)):
                    s = base // 128 + half
                    if s < len(parts):
                        parts[s] = parts[s] + jnp.where(near == numbers, one, zero)
        counts = jnp.concatenate(parts, axis=1)
        out_ref[:, f * width : (f + 1) * width] = jnp.dot(
            counts, table_ref[f], preferred_element_type=jnp.float32
        ).astype(jnp.bfloat16)


def pool(codes, table, bag):
    count = codes.shape[0]
    held, rows_total, width = table.shape
    step = min(256, count)
    return pl.pallas_call(
        lambda c, t, o: pool_kernel(held, bag, c, t, o),
        grid=(count // step,),
        in_specs=[
            pl.BlockSpec((step, held * bag), lambda i: (i, 0)),
            pl.BlockSpec((held, rows_total, width), lambda i: (0, 0, 0)),
        ],
        out_specs=pl.BlockSpec((step, held * width), lambda i: (i, 0)),
        out_shape=jax.ShapeDtypeStruct((count, held * width), jnp.bfloat16),
        cost_estimate=pl.CostEstimate(
            flops=2 * count * held * rows_total * width, bytes_accessed=count * held * width * 2, transcendentals=0
        ),
    )(codes, table)


def on_device(
    cache,
    backing,
    resident,
    promote,
    victim,
    lookups,
    route,
    dcn_down,
    dcn_up,
    dcn_bias,
    mlp_in,
    mlp_bias,
    mlp_out,
    out_bias,
):
    held, slots, block, width = cache.shape
    new_cache, new_backing = promote_blocks(cache, backing, resident, promote, victim)
    codes = routed(lookups, route)
    table = new_cache.reshape(held, slots * block, width)
    x0 = pool(codes, table, lookups.shape[3])
    batches, group = lookups.shape[0], lookups.shape[1]
    here = lax.axis_index("cache")
    devices = lax.axis_size("cache")
    low = lax.psum(jnp.dot(x0, dcn_down, preferred_element_type=jnp.float32), "cache").astype(jnp.bfloat16)
    own_dims = x0.shape[1]
    bias = lax.dynamic_slice_in_dim(dcn_bias, here * own_dims, own_dims, 0)
    gate = jnp.dot(low, dcn_up, preferred_element_type=jnp.float32) + bias
    x1 = (x0 * gate + x0).astype(jnp.bfloat16)
    partial = jnp.dot(x1, mlp_in, preferred_element_type=jnp.float32).astype(jnp.bfloat16)
    per = group // devices
    partial = partial.reshape(batches, devices, per, -1).transpose(1, 0, 2, 3).reshape(devices * batches * per, -1)
    before = lax.psum_scatter(partial, "cache", scatter_dimension=0, tiled=True).astype(jnp.float32)
    hidden = jnp.maximum(before + mlp_bias, 0.0)
    scores = jnp.sum(hidden * mlp_out, axis=-1) + out_bias[0]
    return (scores.reshape(batches, 1, per), new_cache, new_backing)


def solution(mesh):
    in_specs = (
        P("cache", None, None, None),
        P("cache", "owner", None, None),
        P("cache", None),
        P("cache", None),
        P("cache", None),
        P(None, "owner", "cache", None),
        P(None, "owner", None),
        P("cache", None),
        P(None, "cache"),
        P(),
        P("cache", None),
        P(),
        P(),
        P(),
    )
    out_specs = (
        P(None, "owner", "cache"),
        P("cache", None, None, None),
        P("cache", "owner", None, None),
    )
    return jax.shard_map(
        on_device, mesh=mesh, in_specs=in_specs, out_specs=out_specs, check_vma=False
    )
```

time: 393 us -> 241 us (0.61)
  waiting for transfers between devices: 229 us -> 97 us
  blocking collectives: 0 us -> 72.9 us
  local copies, waits for them, and re-layouts: 58.2 us -> 13.3 us
  other arithmetic: 56.9 us -> 13 us
  Pallas kernels: 0 us -> 14.7 us
  starting transfers between devices: 10.3 us -> 0.08 us
  matrix products: 23.8 us -> 14.4 us
    all_gather x5 -> x1, waiting for transfers between devices: 156 us -> 19.2 us  [promote_blocks(): arrived = lax.all_gather(outgoing, 'owner', axis=0, tiled=True)]
    reduce_scatter x0 -> x1, waiting for transfers between devices: none -> 77.8 us  [on_device(): lax.psum_scatter(partial, 'cache', scatter_dimension=0, tiled=True)]
    psum x0 -> x1, blocking collectives: none -> 72.9 us  [on_device(): lax.psum(jnp.dot(x0, dcn_down, preferred_element_type=jnp.float32), 'cache')]
    all_to_all x2 -> x0, waiting for transfers between devices: 71.6 us -> none  [on_device(): lax.all_to_all(pooled, 'cache', split_axis=0, concat_axis=1, tiled=True)]
    reduce_sum x5 -> x2, other arithmetic: 49 us -> 3.42 us  [the longest x1 2.12 us: promote_blocks(): jnp.sum(jnp.where(picked[..., None, None], arrived, jnp.zeros_like(arrive...]
    gather x2 -> x0, local copies, waits for them, and re-layouts: 15.8 us -> none  [pool_batch(): requests = requests[order]]
    pallas_call x0 -> x1, Pallas kernels: none -> 14.7 us  [pool(): pl.pallas_call(lambda c, t, o: pool_kernel(held, bag, c, t, o), grid=(cou...]
    unnamed x31 -> x17, local copies, waits for them, and re-layouts: 15.5 us -> 1.03 us
  transfers between devices with their start and end apart: 7 -> 2, of which waited for: 5 -> 2; matrix products, arithmetic and copies ran while one was open for 31% -> 5% of each run, Pallas kernels for 0% -> 0%
where the time goes in v1:
time: 241 us; the launch traced here: 240 us
  waiting for transfers between devices  97 us (40%)
  blocking collectives  72.9 us (30%)
  between operations  14.9 us (6%)
  Pallas kernels  14.7 us (6%)
  matrix products  14.4 us (6%)
  local copies, waits for them, and re-layouts  13.3 us (6%)
  other arithmetic  13 us (5%)
    reduce_scatter x1, waiting for transfers between devices, on_device(): lax.psum_scatter(partial, 'cache', scatter_dimension=0, tiled=True)  77.8 us
    psum x1, blocking collectives, on_device(): lax.psum(jnp.dot(x0, dcn_down, preferred_element_type=jnp.float32), 'cache')  72.9 us
    all_gather x1, waiting for transfers between devices, promote_blocks(): arrived = lax.all_gather(outgoing, 'owner', axis=0, tiled=True)  19.2 us
    pallas_call x1, Pallas kernels, pool(): pl.pallas_call(lambda c, t, o: pool_kernel(held, bag, c, t, o), grid=(cou...  14.7 us
    dot_general x1, matrix products, on_device(): jnp.dot(x1, mlp_in, preferred_element_type=jnp.float32).astype(jnp.bfloat16)  8.9 us
  transfers between devices with their start and end apart: 2, of which 2 were waited for; matrix products, arithmetic and copies ran while one was open for 5% of the time, Pallas kernels for 0%

profile of v1, /device:TPU:0, one launch (start us, length us, event | category | flops | bytes accessed | tf_op | source)
XLA Modules:
  0.0 240.2 jit_solution(17570628073197838436)
XLA Ops:
  7.2 0.8 fusion.16
  8.1 0.7 compare_and_fusion
  8.7 0.1 copy.35
  8.8 0.1 reshape.140
  8.9 0.1 copy.34
  9.0 2.2 gather_fusion
  11.2 0.9 broadcast_select_fusion
  12.2 0.7 and_select_fusion
  12.9 0.1 copy.33
  13.0 0.7 copy.44
  13.7 1.2 fusion.5
  14.9 2.0 fusion.1
  17.0 1.3 copy.32
  18.4 19.2 %all-gather.2.cloned.1.call-done = bf16[16,2,128,256]{3,2,1,0:T(8,128)(2,1)} async-done(((bf16[4,2,128,256]{3,2,1,0:T(8,128)(2,1)}), bf16[16,2,128,256]{3,2,1,0:T(8,128)(2,1)}) %all-gather.2.cloned.1.call-update) | async-done | bytes 2097168 | tf_op jit(solution)/shard_map/all_gather | solution.py:23
  37.6 2.1 select_reduce_fusion
  39.8 1.2 select_select_fusion.1
  41.0 14.7 %shard_map.157 = bf16[2048,1024]{1,0:T(8,128)(2,1)} custom-call(f32[2048,32]{1,0:T(8,128)} %bitcast.80, bf16[4,512,256]{2,1,0:T(8,128)(2,1)} %bitcast.79), custom_call_target="tpu_custom_call" | custom-call | flops 2147483648 | bytes 4194304 | tf_op jit(solution)/shard_map/pallas_call | solution.py:84
  55.7 3.4 %fusion.22 = f32[2048,128]{1,0:T(8,128)S(1)} fusion(bf16[2048,1024]{1,0:T(8,128)(2,1)} %shard_map.157, bf16[1024,128]{1,0:T(8,128)(2,1)S(1)} %copy-done.4), kind=kOutput, calls=%fused_computation.65 | convolution fusion | flops 536870912 | bytes 5505024 | tf_op jit(solution)/shard_map/dot_general | solution.py:123
  59.1 72.9 %all-reduce.1 = bf16[2048,128]{1,0:T(8,128)(2,1)} all-reduce(f32[2048,128]{1,0:T(8,128)S(1)} %fusion.22), channel_id=1, replica_groups=mesh['cache'=8,'owner'=4] {'cache'}, use_global_device_ids=true, to_apply=%region_1.2 | all-reduce | flops 262144 | bytes 1572864 | tf_op jit(solution)/shard_map/psum | solution.py:123
  132.0 8.9 %convolution_convert_fusion = bf16[2048,1024]{1,0:T(8,128)(2,1)} fusion(bf16[1024,1024]{1,0:T(8,128)(2,1)S(1)} %copy-done, bf16[2048,1024]{1,0:T(8,128)(2,1)} %shard_map.157, bf16[128,1024]{1,0:T(8,128)(2,1)} %param.22, f32[1024]{0:T(1024)S(1)} %dynamic-slice-done, bf16[2048,128]{1,0:T(8,128)(2,1)} %all-reduce.1), kind=kOutput, calls=%fused_computation.8 | convolution fusion | flops 4844421120 | bytes 11276288 | tf_op jit(solution)/shard_map/dot_general | solution.py:128
  140.9 4.7 %copy.36 = bf16[2,8,128,1024]{3,2,0,1:T(8,128)(2,1)} copy(bf16[2,8,128,1024]{3,2,1,0:T(8,128)(2,1)} %bitcast.75) | data formatting | bytes 8388608 | tf_op jit(solution)/shard_map/reshape | solution.py:130
  146.4 0.1 copy.37
  146.5 0.1 reshape.146
  146.6 0.3 copy-done.3
  146.9 1.4 gather_fusion.2
  148.3 0.7 gather_fusion.1
  149.0 0.2 slice_reduce_fusion.1
  149.3 1.1 slice_bitcast_fusion.1
  150.4 3.3 %select_select_fusion = bf16[4,8,128,256]{3,2,1,0:T(8,128)(2,1)} fusion(bf16[4,8,128,256]{3,2,1,0:T(8,128)(2,1)} %param.15, pred[4,8]{1,0:T(4,128)(4,1)S(1)} %get-tuple-element.15, pred[4,8]{1,0:T(4,128)(4,1)S(1)} %get-tuple-element.16, bf16[4,128,256]{2,1,0:T(8,128)(2,1)S(1)} %get-tuple-element.6, bf16[4,128,256]{2,1,0:T(8,128)(2,1)S(1)} %get-tuple-element.5), kind=kLoop, calls=%fused_computation.9 | loop fusion | flops 2097152 | bytes 4718656 | tf_op jit(solution)/shard_map/jit(_where)/select_n | solution.py:39
  153.7 77.8 %reduce-scatter.2.cloned.1.call-done = bf16[256,1024]{1,0:T(8,128)(2,1)} async-done(((bf16[2048,1024]{1,0:T(8,128)(2,1)}), bf16[256,1024]{1,0:T(8,128)(2,1)}) %reduce-scatter.2.cloned.1.call-update) | async-done | bytes 524304 | tf_op jit(solution)/shard_map/reduce_scatter | solution.py:131
  231.5 1.3 multiply_reduce_fusion
  232.8 0.6 broadcast_add_fusion
  (30 shorter events, 0.5 us)
Async XLA Ops:
  7.2 124.9 %copy-start = (bf16[1024,1024]{1,0:T(8,128)(2,1)S(1)}, bf16[1024,1024]{1,0:T(8,128)(2,1)}, u32[]{:S(2)}) copy-start(bf16[1024,1024]{1,0:T(8,128)(2,1)} %param.24) | copy-start | bytes 6291460
  7.2 30.4 %all-gather.2.cloned.1.call-start = ((), (), s32[]{:S(2)}) async-start(), calls=%async_computation.1 | async-start | bytes 2621440 | tf_op jit(solution)/shard_map/all_gather | solution.py:23
  11.2 7.1 %copy-start.7 = (s32[4,2]{0,1:T(2,128)S(1)}, s32[4,2]{0,1:T(2,128)}, u32[]{:S(2)}) copy-start(s32[4,2]{0,1:T(2,128)} %param.18) | copy-start | bytes 100
  12.2 219.3 %reduce-scatter.2.cloned.1.call-start = ((), (), s32[]{:S(2)}) async-start(), calls=%async_computation.2 | async-start | bytes 4718592 | tf_op jit(solution)/shard_map/reduce_scatter | solution.py:131
  14.9 24.9 %copy-start.2 = (bf16[4,4,128,256]{3,2,1,0:T(8,128)(2,1)S(1)}, bf16[4,4,128,256]{3,2,1,0:T(8,128)(2,1)}, u32[]{:S(2)}) copy-start(bf16[4,4,128,256]{3,2,1,0:T(8,128)(2,1)} %param.14) | copy-start | bytes 3145732
  41.0 14.7 %copy-start.4 = (bf16[1024,128]{1,0:T(8,128)(2,1)S(1)}, bf16[1024,128]{1,0:T(8,128)(2,1)}, u32[]{:S(2)}) copy-start(bf16[1024,128]{1,0:T(8,128)(2,1)} %param.21) | copy-start | bytes 786436
  55.7 76.4 %dynamic-slice-start = ((f32[8192]{0:T(1024)}, s32[]{:T(128)}), f32[1024]{0:T(1024)S(1)}, s32[]{:S(2)}) async-start(f32[8192]{0:T(1024)} %param.23, s32[]{:T(128)} %select_n.57), calls=%async_computation.3 | async-start | bytes 8704 | tf_op jit(solution)/shard_map/dynamic_slice | solution.py:125
  145.7 1.2 copy-start.3
  145.7 2.6 %copy-start.1 = (s32[4,4]{1,0:T(4,128)S(1)}, s32[4,4]{1,0:T(4,128)}, u32[]{:S(2)}) copy-start(s32[4,4]{1,0:T(4,128)} %param.16) | copy-start | bytes 196
  148.3 83.2 %copy-start.5 = (f32[1024]{0:T(1024)S(1)}, f32[1024]{0:T(1024)}, u32[]{:S(2)}) copy-start(f32[1024]{0:T(1024)} %param.26) | copy-start | bytes 12292
  148.3 83.2 %copy-start.6 = (f32[1024]{0:T(1024)S(1)}, f32[1024]{0:T(1024)}, u32[]{:S(2)}) copy-start(f32[1024]{0:T(1024)} %param.25) | copy-start | bytes 12292
Sparse Core Ops, SparseCore 0:
  12.3 25.2 all-gather.1
  145.8 85.6 reduce-scatter.1

commit v2 on v1

--- a/solution.py
+++ b/solution.py
@@ -42,14 +42,15 @@
     return new_cache, new_backing
 
 
-def routed(lookups, route):
+def routed(lookups, route, devices):
     batches, count, held, bag = lookups.shape
     flat = lookups.reshape(batches, count, held * bag)
     halves = jnp.concatenate([flat // 256, flat % 256], axis=-1).astype(jnp.bfloat16)
     pick = (route[:, 0, :, None] == jnp.arange(count, dtype=jnp.int32)).astype(jnp.bfloat16)
     got = jnp.einsum("bpr,brj->bpj", pick, halves, preferred_element_type=jnp.float32)
     upper, lower = jnp.split(got, 2, axis=-1)
-    return (upper * 256.0 + lower).reshape(batches * count, held * bag)
+    codes = (upper * 256.0 + lower).reshape(batches, devices, count // devices, held * bag)
+    return codes.transpose(1, 0, 2, 3).reshape(batches * count, held * bag)
 
 
 def pool_kernel(held, bag, codes_ref, table_ref, out_ref):
@@ -96,6 +97,159 @@
     )(codes, table)
 
 
+def dense_kernel(
+    n,
+    x0_ref,
+    down_ref,
+    up_ref,
+    bias_ref,
+    w_ref,
+    mlp_bias_ref,
+    mlp_out_ref,
+    out_bias_ref,
+    scores_ref,
+    low_send,
+    low_recv,
+    low_full,
+    near_send,
+    near_recv,
+    far_send,
+    far_recv,
+    total_ref,
+    low_sems,
+    full_sems,
+    near_sems,
+    far_sems,
+):
+    rows = x0_ref.shape[0] // n
+    pair = 2 if n % 2 == 0 else 1
+    lines = n // pair
+    me = lax.axis_index("cache")
+    line, side = me // pair, me % pair
+
+    def at(c):
+        return pl.ds(pl.multiple_of(c * rows, rows), rows)
+
+    def send(src, dst, sems, k, c):
+        copy = pltpu.make_async_remote_copy(
+            src_ref=src,
+            dst_ref=dst,
+            send_sem=sems.at[0, k],
+            recv_sem=sems.at[1, k],
+            device_id={"cache": c},
+            device_id_type=pl.DeviceIdType.MESH,
+        )
+        copy.start()
+        return copy
+
+    def dense(c):
+        x0 = x0_ref[at(c), :]
+        gate = jnp.dot(low_full[c], up_ref[...], preferred_element_type=jnp.float32) + bias_ref[...]
+        wide = x0.astype(jnp.float32)
+        x1 = (wide * gate + wide).astype(jnp.bfloat16)
+        return jnp.dot(x1, w_ref[...], preferred_element_type=jnp.float32)
+
+    barrier = pltpu.get_barrier_semaphore()
+    for o in range(1, n):
+        pl.semaphore_signal(
+            barrier, inc=1, device_id={"cache": lax.rem(me + o, n)}, device_id_type=pl.DeviceIdType.MESH
+        )
+    pl.semaphore_wait(barrier, n - 1)
+
+    copies = []
+    for o in range(1, n):
+        c = lax.rem(me + o, n)
+        low_send[o - 1] = jnp.dot(
+            x0_ref[at(c), :], down_ref[...], preferred_element_type=jnp.float32
+        ).astype(jnp.bfloat16)
+        copies.append(send(low_send.at[o - 1], low_recv.at[o - 1], low_sems, o - 1, c))
+    low = jnp.dot(x0_ref[at(me), :], down_ref[...], preferred_element_type=jnp.float32)
+    for o in range(1, n):
+        copies[o - 1].wait_recv()
+        low = low + low_recv[o - 1].astype(jnp.float32)
+    low_full[me] = low.astype(jnp.bfloat16)
+    shares = [
+        send(low_full.at[me], low_full.at[me], full_sems, o - 1, lax.rem(me + o, n)) for o in range(1, n)
+    ]
+    for copy in shares:
+        copy.wait_recv()
+
+    offsets = list(range(1, lines)) + [0]
+    nears, fars = [], []
+
+    def first(k):
+        c = lax.rem(line + offsets[k], lines) * pair + (pair - 1 - side)
+        near_send[k] = dense(c).astype(jnp.bfloat16)
+        nears.append(send(near_send.at[k], near_recv.at[k], near_sems, k, line * pair + (pair - 1 - side)))
+
+    def second(k):
+        c = lax.rem(line + offsets[k], lines) * pair + side
+        part = dense(c)
+        if pair > 1:
+            nears[k].wait_recv()
+            part = part + near_recv[k].astype(jnp.float32)
+        if offsets[k]:
+            far_send[k] = part.astype(jnp.bfloat16)
+            fars.append(send(far_send.at[k], far_recv.at[k], far_sems, k, c))
+        else:
+            total_ref[...] = part
+
+    for k in range(lines + 1):
+        if k < lines and pair > 1:
+            first(k)
+        if k:
+            second(k - 1)
+    total = total_ref[...]
+    for k, copy in enumerate(fars):
+        copy.wait_recv()
+        total = total + far_recv[k].astype(jnp.float32)
+    hidden = jnp.maximum(total + mlp_bias_ref[...], 0.0)
+    scores_ref[...] = jnp.sum(hidden * mlp_out_ref[...], axis=1, keepdims=True) + out_bias_ref[...]
+    for copy in copies + shares + nears + fars:
+        copy.wait_send()
+
+
+def dense_stack(x0, down, up, bias, w, mlp_bias, mlp_out, out_bias):
+    n = lax.axis_size("cache")
+    rows = x0.shape[0] // n
+    rank, hid = down.shape[1], w.shape[1]
+    lines = n // 2 if n % 2 == 0 else n
+    fars = max(lines - 1, 1)
+    vmem = pl.BlockSpec(memory_space=pltpu.VMEM)
+    return pl.pallas_call(
+        lambda *refs: dense_kernel(n, *refs),
+        in_specs=[vmem] * 8,
+        out_specs=vmem,
+        out_shape=jax.ShapeDtypeStruct((rows, 1), jnp.float32),
+        scratch_shapes=[
+            pltpu.VMEM((n - 1, rows, rank), jnp.bfloat16),
+            pltpu.VMEM((n - 1, rows, rank), jnp.bfloat16),
+            pltpu.VMEM((n, rows, rank), jnp.bfloat16),
+            pltpu.VMEM((lines, rows, hid), jnp.bfloat16),
+            pltpu.VMEM((lines, rows, hid), jnp.bfloat16),
+            pltpu.VMEM((fars, rows, hid), jnp.bfloat16),
+            pltpu.VMEM((fars, rows, hid), jnp.bfloat16),
+            pltpu.VMEM((rows, hid), jnp.float32),
+            pltpu.SemaphoreType.DMA((2, n - 1)),
+            pltpu.SemaphoreType.DMA((2, n - 1)),
+            pltpu.SemaphoreType.DMA((2, lines)),
+            pltpu.SemaphoreType.DMA((2, fars)),
+        ],
+        compiler_params=pltpu.CompilerParams(
+            collective_id=0, has_side_effects=True, vmem_limit_bytes=60 * 1024 * 1024
+        ),
+    )(
+        x0,
+        down,
+        up,
+        bias.reshape(1, -1),
+        w,
+        mlp_bias.reshape(1, -1),
+        mlp_out.reshape(1, -1),
+        out_bias.reshape(1, 1),
+    )
+
+
 def on_device(
     cache,
     backing,
@@ -114,23 +268,16 @@
 ):
     held, slots, block, width = cache.shape
     new_cache, new_backing = promote_blocks(cache, backing, resident, promote, victim)
-    codes = routed(lookups, route)
+    codes = routed(lookups, route, lax.axis_size("cache"))
     table = new_cache.reshape(held, slots * block, width)
     x0 = pool(codes, table, lookups.shape[3])
     batches, group = lookups.shape[0], lookups.shape[1]
     here = lax.axis_index("cache")
     devices = lax.axis_size("cache")
-    low = lax.psum(jnp.dot(x0, dcn_down, preferred_element_type=jnp.float32), "cache").astype(jnp.bfloat16)
     own_dims = x0.shape[1]
     bias = lax.dynamic_slice_in_dim(dcn_bias, here * own_dims, own_dims, 0)
-    gate = jnp.dot(low, dcn_up, preferred_element_type=jnp.float32) + bias
-    x1 = (x0 * gate + x0).astype(jnp.bfloat16)
-    partial = jnp.dot(x1, mlp_in, preferred_element_type=jnp.float32).astype(jnp.bfloat16)
     per = group // devices
-    partial = partial.reshape(batches, devices, per, -1).transpose(1, 0, 2, 3).reshape(devices * batches * per, -1)
-    before = lax.psum_scatter(partial, "cache", scatter_dimension=0, tiled=True).astype(jnp.float32)
-    hidden = jnp.maximum(before + mlp_bias, 0.0)
-    scores = jnp.sum(hidden * mlp_out, axis=-1) + out_bias[0]
+    scores = dense_stack(x0, dcn_down, dcn_up, bias, mlp_in, mlp_bias, mlp_out, out_bias)
     return (scores.reshape(batches, 1, per), new_cache, new_backing)
 
 

time: 241 us -> 160 us (0.66)
  Pallas kernels: 14.7 us -> 109 us
  waiting for transfers between devices: 97 us -> 14.2 us
  blocking collectives: 72.9 us -> 0 us
  matrix products: 14.4 us -> 2.03 us
  local copies, waits for them, and re-layouts: 13.3 us -> 8.88 us
  other arithmetic: 13 us -> 9.32 us
    pallas_call x0 -> x1, Pallas kernels: none -> 94.1 us  [dense_stack(): pl.pallas_call(lambda *refs: dense_kernel(n, *refs), in_specs=[vmem] * 8,...]
    reduce_scatter x1 -> x0, waiting for transfers between devices: 77.8 us -> none  [on_device(): lax.psum_scatter(partial, 'cache', scatter_dimension=0, tiled=True)]
    psum x1 -> x0, blocking collectives: 72.9 us -> none  [on_device(): lax.psum(jnp.dot(x0, dcn_down, preferred_element_type=jnp.float32), 'cache')]
    dot_general x2 -> x0, matrix products: 12.3 us -> none  [the longest x1 8.9 us: on_device(): jnp.dot(x1, mlp_in, preferred_element_type=jnp.float32).astype(jnp.bfloat16)]
    all_gather x1, waiting for transfers between devices: 19.2 us -> 14.2 us  [promote_blocks(): arrived = lax.all_gather(outgoing, 'owner', axis=0, tiled=True)]
    reshape x1, local copies, waits for them, and re-layouts: 4.72 us -> 1.34 us  [routed(): (upper * 256.0 + lower).reshape(batches, devices, count // devices, held...]
  transfers between devices with their start and end apart: 2 -> 1, of which waited for: 2 -> 1; matrix products, arithmetic and copies ran while one was open for 5% -> 7% of each run, Pallas kernels for 0% -> 0%
where the time goes in v2:
time: 160 us; the launch traced here: 158 us
  Pallas kernels  109 us (68%)
  between operations  14.9 us (9%)
  waiting for transfers between devices  14.2 us (9%)
  other arithmetic  9.32 us (6%)
  local copies, waits for them, and re-layouts  8.88 us (6%)
  matrix products  2.03 us (1%)
    pallas_call x1, Pallas kernels, dense_stack(): pl.pallas_call(lambda *refs: dense_kernel(n, *refs), in_specs=[vmem] * 8,...  94.1 us
    pallas_call x1, Pallas kernels, pool(): pl.pallas_call(lambda c, t, o: pool_kernel(held, bag, c, t, o), grid=(cou...  14.6 us
    all_gather x1, waiting for transfers between devices, promote_blocks(): arrived = lax.all_gather(outgoing, 'owner', axis=0, tiled=True)  14.2 us
    gather x7, local copies, waits for them, and re-layouts, take_rows(): return jax.vmap(lambda rows, chosen: rows[chosen])(table, wanted)  4.57 us
  transfers between devices with their start and end apart: 1, of which 1 were waited for; matrix products, arithmetic and copies ran while one was open for 7% of the time, Pallas kernels for 0%

profile of v2, /device:TPU:0, one launch (start us, length us, event | category | flops | bytes accessed | tf_op | source)
XLA Modules:
  0.0 158.1 jit_solution(3258061266680764403)
XLA Ops:
  7.2 0.0 copy-start
  7.2 0.0 copy-start.4
  7.2 0.0 all-gather.2.cloned.1.call-start
  7.3 0.7 fusion.13
  8.0 0.7 compare_and_fusion
  8.7 0.1 copy.36
  8.8 0.1 reshape.140
  8.9 0.1 copy.35
  9.0 2.2 %gather_fusion = bf16[8,128,256]{2,1,0:T(8,128)(2,1)S(1)} fusion(bf16[4,8,128,256]{3,2,1,0:T(8,128)(2,1)} %param.15, s32[8]{0:T(128)S(1)} %reshape.140), kind=kCustom, calls=%fused_computation | custom fusion | bytes 1048640 | tf_op jit(solution)/shard_map/vmap()/gather | solution.py:10
  11.1 0.9 broadcast_select_fusion
  12.0 0.0 all-gather.2.cloned.1.call-update
  12.1 0.1 copy.34
  12.2 0.3 fusion.2
  12.5 2.0 %fusion = f32[2,1024,64]{1,2,0:T(8,128)S(1)} fusion(s32[2,1024]{1,0:T(2,128)S(1)} %bitcast.86, bf16[2,1024,32]{1,2,0:T(8,128)(2,1)S(1)} %get-tuple-element.19, bf16[2,1024,32]{1,2,0:T(8,128)(2,1)S(1)} %get-tuple-element.18), kind=kOutput, calls=%fused_computation.4 | convolution fusion | flops 271056896 | bytes 794624 | tf_op jit(solution)/shard_map/bpr,brj->bpj/dot_general | solution.py:50
  14.6 1.3 copy.33
  16.6 0.1 copy.37
  16.7 0.1 reshape.146
  16.8 0.7 gather_fusion.1
  17.5 0.1 reshape.159
  17.6 1.4 gather_fusion.2
  19.0 1.3 dynamic_slice.3
  20.2 0.2 slice_reduce_fusion.1
  20.4 0.1 iota_compare_fusion.5
  20.5 0.1 iota_compare_fusion.3
  20.6 1.1 slice_bitcast_fusion.1
  21.7 1.7 %select_select_fusion = bf16[4,8,128,256]{3,2,1,0:T(8,128)(2,1)} fusion(bf16[4,8,128,256]{3,2,1,0:T(8,128)(2,1)S(1)} %copy-done.1, pred[4,8]{1,0:T(4,128)(4,1)S(1)} %get-tuple-element.24, pred[4,8]{1,0:T(4,128)(4,1)S(1)} %get-tuple-element.25, bf16[4,128,256]{2,1,0:T(8,128)(2,1)S(1)} %get-tuple-element.15, bf16[4,128,256]{2,1,0:T(8,128)(2,1)S(1)} %get-tuple-element.14), kind=kLoop, calls=%fused_computation.6 | loop fusion | flops 2097152 | bytes 4718656 | tf_op jit(solution)/shard_map/jit(_where)/select_n | solution.py:39
  23.3 14.2 %all-gather.2.cloned.1.call-done = bf16[16,2,128,256]{3,2,1,0:T(8,128)(2,1)} async-done(((bf16[4,2,128,256]{3,2,1,0:T(8,128)(2,1)}), bf16[16,2,128,256]{3,2,1,0:T(8,128)(2,1)}) %all-gather.2.cloned.1.call-update) | async-done | bytes 2097168 | tf_op jit(solution)/shard_map/all_gather | solution.py:23
  37.5 2.1 %select_reduce_fusion = bf16[4,2,128,256]{3,2,1,0:T(8,128)(2,1)S(1)} fusion(bf16[4,4,2,128,256]{4,3,2,1,0:T(8,128)(2,1)} %bitcast.78, pred[4,4,2]{2,1,0:T(4,128)(4,1)S(1)} %iota_compare_fusion.2), kind=kLoop, calls=%fused_computation.7 | loop fusion | flops 1835008 | bytes 2621472 | tf_op jit(solution)/shard_map/reduce_sum | solution.py:28
  39.7 1.2 select_select_fusion.1
  40.9 14.6 %shard_map.157.refs_0_ = bf16[2048,1024]{1,0:T(8,128)(2,1)} custom-call(f32[2048,32]{1,0:T(8,128)} %bitcast.82, bf16[4,512,256]{2,1,0:T(8,128)(2,1)} %bitcast.81), custom_call_target="tpu_custom_call" | custom-call | flops 2147483648 | bytes 4194304 | tf_op jit(solution)/shard_map/pallas_call | solution.py:85
  55.5 94.1 %shard_map.158 = f32[256,1]{1,0:T(8,128)} custom-call(bf16[2048,1024]{1,0:T(8,128)(2,1)} %shard_map.157.refs_0_, bf16[1024,128]{1,0:T(8,128)(2,1)} %refs_1_.1, bf16[128,1024]{1,0:T(8,128)(2,1)} %refs_2_.1, f32[1,1024]{1,0:T(1,128)} %bitcast.85, bf16[1024,1024]{1,0:T(8,128)(2,1)} %refs_4_.1, f32[1,1024]{1,0:T(1,128)} %bitcast.87, f32[1,1024]{1,0:T(1,128)} %bitcast.88, ...), custom_call_target="tpu_custom_call" | custom-call | tf_op jit(solution)/shard_map/pallas_call | solution.py:219
  149.7 1.6 %reduce.1 = f32[256]{0:T(256)} reduce(f32[256,1]{1,0:T(8,128)} %shard_map.158, f32[]{:T(128)} %constant.113), dimensions={1}, to_apply=%pallas_call.7.reduce_sub_computation | reduce | bytes 2052 | tf_op jit(solution)/shard_map/pallas_call | solution.py:219
  (21 shorter events, 0.2 us)
Async XLA Ops:
  7.2 9.7 %copy-start = (s32[4,4]{1,0:T(4,128)S(1)}, s32[4,4]{1,0:T(4,128)}, u32[]{:S(2)}) copy-start(s32[4,4]{1,0:T(4,128)} %param.16) | copy-start | bytes 196
  7.2 4.9 %copy-start.4 = (s32[4,2]{0,1:T(2,128)S(1)}, s32[4,2]{0,1:T(2,128)}, u32[]{:S(2)}) copy-start(s32[4,2]{0,1:T(2,128)} %param.17) | copy-start | bytes 100
  7.2 5.0 %copy-start.5 = (s32[2,1,1024]{2,1,0:T(1,128)S(1)}, s32[2,1,1024]{2,1,0:T(1,128)}, u32[]{:S(2)}) copy-start(s32[2,1,1024]{2,1,0:T(1,128)} %param.20) | copy-start | bytes 24580
  7.2 5.0 %copy-start.3 = (s32[2,1024,4,8]{1,3,2,0:T(8,128)S(1)}, s32[2,1024,4,8]{1,3,2,0:T(8,128)}, u32[]{:S(2)}) copy-start(s32[2,1024,4,8]{1,3,2,0:T(8,128)} %param.19) | copy-start | bytes 786436
  7.2 30.3 %all-gather.2.cloned.1.call-start = ((), (), s32[]{:S(2)}) async-start(), calls=%async_computation | async-start | bytes 2621440 | tf_op jit(solution)/shard_map/all_gather | solution.py:23
  14.5 2.1 %copy-start.6 = (s32[4,2]{0,1:T(2,128)S(1)}, s32[4,2]{0,1:T(2,128)}, u32[]{:S(2)}) copy-start(s32[4,2]{0,1:T(2,128)} %param.18) | copy-start | bytes 100
  14.6 3.0 %copy-start.2 = (bf16[4,4,128,256]{3,2,1,0:T(8,128)(2,1)S(1)}, bf16[4,4,128,256]{3,2,1,0:T(8,128)(2,1)}, u32[]{:S(2)}) copy-start(bf16[4,4,128,256]{3,2,1,0:T(8,128)(2,1)} %param.14) | copy-start | bytes 3145732
  16.8 4.9 %copy-start.1 = (bf16[4,8,128,256]{3,2,1,0:T(8,128)(2,1)S(1)}, bf16[4,8,128,256]{3,2,1,0:T(8,128)(2,1)}, u32[]{:S(2)}) copy-start(bf16[4,8,128,256]{3,2,1,0:T(8,128)(2,1)} %param.15) | copy-start | bytes 6291460
Sparse Core Ops, SparseCore 0:
  12.2 25.2 all-gather.1

commit v3 on v2

--- a/solution.py
+++ b/solution.py
@@ -8,6 +8,86 @@
 
 def take_rows(table, wanted):
     return jax.vmap(lambda rows, chosen: rows[chosen])(table, wanted)
+
+
+def gather_kernel(n, mine_ref, out_ref, near_recv, far_send, far_recv, done_send, done_recv, near_sems, far_sems):
+    pair = out_ref.shape[0] // far_send.shape[0]
+    lines = n // pair
+    part = far_send.shape[0]
+    me = lax.axis_index("owner")
+    line, side = me // pair, me % pair
+    buddy = line * pair + (pair - 1 - side)
+    own, other = pl.ds(side * part, part), pl.ds((pair - 1 - side) * part, part)
+
+    def send(src, dst, send_sem, recv_sem, c):
+        copy = pltpu.make_async_remote_copy(
+            src_ref=src,
+            dst_ref=dst,
+            send_sem=send_sem,
+            recv_sem=recv_sem,
+            device_id={"owner": c},
+            device_id_type=pl.DeviceIdType.MESH,
+        )
+        copy.start()
+        return copy
+
+    across = [lax.rem(line + o, lines) * pair + side for o in range(1, lines)]
+    peers = across + ([buddy] if pair > 1 else [])
+    barrier = pltpu.get_barrier_semaphore()
+    for c in peers:
+        pl.semaphore_signal(barrier, inc=1, device_id={"owner": c}, device_id_type=pl.DeviceIdType.MESH)
+    pl.semaphore_wait(barrier, len(peers))
+
+    copies = []
+    total = mine_ref[own]
+    if pair > 1:
+        copy = send(mine_ref.at[other], near_recv, near_sems.at[0, 0], near_sems.at[1, 0], buddy)
+        copy.wait_recv()
+        total = total + near_recv[...]
+        copies.append(copy)
+    far_send[...] = total
+    fars = [
+        send(far_send, far_recv.at[k], far_sems.at[0, k], far_sems.at[1, k], c) for k, c in enumerate(across)
+    ]
+    for k, copy in enumerate(fars):
+        copy.wait_recv()
+        total = total + far_recv[k]
+    out_ref[own] = total
+    if pair > 1:
+        done_send[...] = total
+        copy = send(done_send, done_recv, near_sems.at[0, 1], near_sems.at[1, 1], buddy)
+        copy.wait_recv()
+        out_ref[other] = done_recv[...]
+        copies.append(copy)
+    for copy in copies + fars:
+        copy.wait_send()
+
+
+def everywhere(outgoing):
+    n = lax.axis_size("owner")
+    held, promoted_count, block, width = outgoing.shape
+    blocks = held * promoted_count
+    pair = 2 if n % 2 == 0 and blocks % 2 == 0 else 1
+    part = (blocks // pair, block, width)
+    fars = max(n // pair - 1, 1)
+    vmem = pl.BlockSpec(memory_space=pltpu.VMEM)
+    got = pl.pallas_call(
+        lambda *refs: gather_kernel(n, *refs),
+        in_specs=[vmem],
+        out_specs=vmem,
+        out_shape=jax.ShapeDtypeStruct((blocks, block, width), outgoing.dtype),
+        scratch_shapes=[
+            pltpu.VMEM(part, outgoing.dtype),
+            pltpu.VMEM(part, outgoing.dtype),
+            pltpu.VMEM((fars,) + part, outgoing.dtype),
+            pltpu.VMEM(part, outgoing.dtype),
+            pltpu.VMEM(part, outgoing.dtype),
+            pltpu.SemaphoreType.DMA((2, 2)),
+            pltpu.SemaphoreType.DMA((2, fars)),
+        ],
+        compiler_params=pltpu.CompilerParams(collective_id=1, has_side_effects=True),
+    )(outgoing.reshape(blocks, block, width))
+    return got.reshape(outgoing.shape)
 
 
 def promote_blocks(cache, backing, resident, promote, victim):
@@ -20,12 +100,7 @@
     clamped = jnp.clip(local_index, 0, own_blocks - 1)
     fetched = take_rows(backing, clamped)
     outgoing = jnp.where(owned_here[:, :, None, None], fetched, jnp.zeros_like(fetched))
-    arrived = lax.all_gather(outgoing, "owner", axis=0, tiled=True)
-    owners = arrived.shape[0] // held
-    arrived = arrived.reshape(owners, held, promoted_count, block, width)
-    source = promote // own_blocks
-    picked = source[None] == jnp.arange(owners, dtype=jnp.int32)[:, None, None]
-    promoted = jnp.sum(jnp.where(picked[..., None, None], arrived, jnp.zeros_like(arrived)), axis=0)
+    promoted = everywhere(outgoing)
     evicted = take_rows(cache, victim)
     leaving = take_rows(resident, victim) - owner_here * own_blocks
     slot_numbers = jnp.arange(slots, dtype=jnp.int32)
@@ -53,19 +128,20 @@
     return codes.transpose(1, 0, 2, 3).reshape(batches * count, held * bag)
 
 
-def pool_kernel(held, bag, codes_ref, table_ref, out_ref):
-    rows_total, width = table_ref.shape[1], table_ref.shape[2]
-    step = codes_ref.shape[0]
+def pool_rows(codes, table_ref, bag):
+    held, rows_total, width = table_ref.shape
+    step = codes.shape[0]
     lane = lax.broadcasted_iota(jnp.int32, (step, 128), 1).astype(jnp.float32)
     low_lane = lane.astype(jnp.bfloat16)
     high_lane = (lane + 128.0).astype(jnp.bfloat16)
     one = jnp.ones((step, 128), jnp.bfloat16)
     zero = jnp.zeros((step, 128), jnp.bfloat16)
+    pooled = []
     for f in range(held):
         parts = [zero] * (rows_total // 128)
         for l in range(bag):
             j = f * bag + l
-            spread = jnp.broadcast_to(codes_ref[:, j : j + 1], (step, 128))
+            spread = jnp.broadcast_to(codes[:, j : j + 1], (step, 128))
             for base in range(0, rows_total, 256):
                 near = (spread - float(base)).astype(jnp.bfloat16)
                 for half, numbers in enumerate((low_lane, high_lane)):
@@ -73,33 +149,17 @@
                     if s < len(parts):
                         parts[s] = parts[s] + jnp.where(near == numbers, one, zero)
         counts = jnp.concatenate(parts, axis=1)
-        out_ref[:, f * width : (f + 1) * width] = jnp.dot(
-            counts, table_ref[f], preferred_element_type=jnp.float32
-        ).astype(jnp.bfloat16)
-
-
-def pool(codes, table, bag):
-    count = codes.shape[0]
-    held, rows_total, width = table.shape
-    step = min(256, count)
-    return pl.pallas_call(
-        lambda c, t, o: pool_kernel(held, bag, c, t, o),
-        grid=(count // step,),
-        in_specs=[
-            pl.BlockSpec((step, held * bag), lambda i: (i, 0)),
-            pl.BlockSpec((held, rows_total, width), lambda i: (0, 0, 0)),
-        ],
-        out_specs=pl.BlockSpec((step, held * width), lambda i: (i, 0)),
-        out_shape=jax.ShapeDtypeStruct((count, held * width), jnp.bfloat16),
-        cost_estimate=pl.CostEstimate(
-            flops=2 * count * held * rows_total * width, bytes_accessed=count * held * width * 2, transcendentals=0
-        ),
-    )(codes, table)
+        pooled.append(
+            jnp.dot(counts, table_ref[f], preferred_element_type=jnp.float32).astype(jnp.bfloat16)
+        )
+    return jnp.concatenate(pooled, axis=1)
 
 
 def dense_kernel(
     n,
-    x0_ref,
+    bag,
+    codes_ref,
+    table_ref,
     down_ref,
     up_ref,
     bias_ref,
@@ -108,6 +168,8 @@
     mlp_out_ref,
     out_bias_ref,
     scores_ref,
+    x0_ref,
+    low_ref,
     low_send,
     low_recv,
     low_full,
@@ -130,8 +192,8 @@
     def at(c):
         return pl.ds(pl.multiple_of(c * rows, rows), rows)
 
-    def send(src, dst, sems, k, c):
-        copy = pltpu.make_async_remote_copy(
+    def to(src, dst, sems, k, c):
+        return pltpu.make_async_remote_copy(
             src_ref=src,
             dst_ref=dst,
             send_sem=sems.at[0, k],
@@ -139,8 +201,15 @@
             device_id={"cache": c},
             device_id_type=pl.DeviceIdType.MESH,
         )
+
+    def send(*args):
+        copy = to(*args)
         copy.start()
         return copy
+
+    def await_low(c):
+        k = lax.rem(me - c + n, n) - 1
+        to(low_full.at[c], low_full.at[c], full_sems, k, c).wait_recv()
 
     def dense(c):
         x0 = x0_ref[at(c), :]
@@ -156,14 +225,26 @@
         )
     pl.semaphore_wait(barrier, n - 1)
 
-    copies = []
-    for o in range(1, n):
+    @pl.loop(1, n + 1)
+    def _(o):
         c = lax.rem(me + o, n)
-        low_send[o - 1] = jnp.dot(
-            x0_ref[at(c), :], down_ref[...], preferred_element_type=jnp.float32
-        ).astype(jnp.bfloat16)
-        copies.append(send(low_send.at[o - 1], low_recv.at[o - 1], low_sems, o - 1, c))
-    low = jnp.dot(x0_ref[at(me), :], down_ref[...], preferred_element_type=jnp.float32)
+        x0 = pool_rows(codes_ref[at(c), :], table_ref, bag)
+        x0_ref[at(c), :] = x0
+        low = jnp.dot(x0, down_ref[...], preferred_element_type=jnp.float32)
+
+        @pl.when(o < n)
+        def _():
+            low_send[o - 1] = low.astype(jnp.bfloat16)
+            send(low_send.at[o - 1], low_recv.at[o - 1], low_sems, o - 1, c)
+
+        @pl.when(o == n)
+        def _():
+            low_ref[...] = low
+
+    low = low_ref[...]
+    copies = [
+        to(low_send.at[o - 1], low_recv.at[o - 1], low_sems, o - 1, lax.rem(me + o, n)) for o in range(1, n)
+    ]
     for o in range(1, n):
         copies[o - 1].wait_recv()
         low = low + low_recv[o - 1].astype(jnp.float32)
@@ -171,19 +252,20 @@
     shares = [
         send(low_full.at[me], low_full.at[me], full_sems, o - 1, lax.rem(me + o, n)) for o in range(1, n)
     ]
-    for copy in shares:
-        copy.wait_recv()
 
     offsets = list(range(1, lines)) + [0]
     nears, fars = [], []
 
     def first(k):
         c = lax.rem(line + offsets[k], lines) * pair + (pair - 1 - side)
+        await_low(c)
         near_send[k] = dense(c).astype(jnp.bfloat16)
         nears.append(send(near_send.at[k], near_recv.at[k], near_sems, k, line * pair + (pair - 1 - side)))
 
     def second(k):
         c = lax.rem(line + offsets[k], lines) * pair + side
+        if offsets[k]:
+            await_low(c)
         part = dense(c)
         if pair > 1:
             nears[k].wait_recv()
@@ -209,19 +291,21 @@
         copy.wait_send()
 
 
-def dense_stack(x0, down, up, bias, w, mlp_bias, mlp_out, out_bias):
+def dense_stack(codes, table, bag, down, up, bias, w, mlp_bias, mlp_out, out_bias):
     n = lax.axis_size("cache")
-    rows = x0.shape[0] // n
+    rows = codes.shape[0] // n
     rank, hid = down.shape[1], w.shape[1]
     lines = n // 2 if n % 2 == 0 else n
     fars = max(lines - 1, 1)
     vmem = pl.BlockSpec(memory_space=pltpu.VMEM)
     return pl.pallas_call(
-        lambda *refs: dense_kernel(n, *refs),
-        in_specs=[vmem] * 8,
+        lambda *refs: dense_kernel(n, bag, *refs),
+        in_specs=[vmem] * 9,
         out_specs=vmem,
         out_shape=jax.ShapeDtypeStruct((rows, 1), jnp.float32),
         scratch_shapes=[
+            pltpu.VMEM((n * rows, down.shape[0]), jnp.bfloat16),
+            pltpu.VMEM((rows, rank), jnp.float32),
             pltpu.VMEM((n - 1, rows, rank), jnp.bfloat16),
             pltpu.VMEM((n - 1, rows, rank), jnp.bfloat16),
             pltpu.VMEM((n, rows, rank), jnp.bfloat16),
@@ -239,7 +323,8 @@
             collective_id=0, has_side_effects=True, vmem_limit_bytes=60 * 1024 * 1024
         ),
     )(
-        x0,
+        codes,
+        table,
         down,
         up,
         bias.reshape(1, -1),
@@ -270,14 +355,13 @@
     new_cache, new_backing = promote_blocks(cache, backing, resident, promote, victim)
     codes = routed(lookups, route, lax.axis_size("cache"))
     table = new_cache.reshape(held, slots * block, width)
-    x0 = pool(codes, table, lookups.shape[3])
     batches, group = lookups.shape[0], lookups.shape[1]
     here = lax.axis_index("cache")
     devices = lax.axis_size("cache")
-    own_dims = x0.shape[1]
+    own_dims = dcn_down.shape[0]
     bias = lax.dynamic_slice_in_dim(dcn_bias, here * own_dims, own_dims, 0)
     per = group // devices
-    scores = dense_stack(x0, dcn_down, dcn_up, bias, mlp_in, mlp_bias, mlp_out, out_bias)
+    scores = dense_stack(codes, table, lookups.shape[3], dcn_down, dcn_up, bias, mlp_in, mlp_bias, mlp_out, out_bias)
     return (scores.reshape(batches, 1, per), new_cache, new_backing)
 
 

time: 160 us -> 134 us (0.84)
  waiting for transfers between devices: 14.2 us -> 0 us
  between operations: 14.9 us -> 1.47 us
  Pallas kernels: 109 us -> 111 us
    all_gather x1 -> x0, waiting for transfers between devices: 14.2 us -> none  [promote_blocks(): arrived = lax.all_gather(outgoing, 'owner', axis=0, tiled=True)]
    pallas_call x2, Pallas kernels: 109 us -> 111 us  [the longest x1 97.2 us: dense_stack(): pl.pallas_call(lambda *refs: dense_kernel(n, bag, *refs), in_specs=[vmem]...]
    reduce_sum x1 -> x0, other arithmetic: 2.12 us -> none  [promote_blocks(): jnp.sum(jnp.where(picked[..., None, None], arrived, jnp.zeros_like(arrive...]
  transfers between devices with their start and end apart: 1 -> 0, of which waited for: 1 -> 0; matrix products, arithmetic and copies ran while one was open for 7% -> 0% of each run, Pallas kernels for 0% -> 0%
where the time goes in v3:
time: 134 us
  Pallas kernels  111 us (83%)
  local copies, waits for them, and re-layouts  9.88 us (7%)
  other arithmetic  8.85 us (7%)
  matrix products  2.03 us (2%)
  between operations  1.47 us (1%)
    pallas_call x1, Pallas kernels, dense_stack(): pl.pallas_call(lambda *refs: dense_kernel(n, bag, *refs), in_specs=[vmem]...  97.2 us
    pallas_call x1, Pallas kernels, everywhere(): pl.pallas_call(lambda *refs: gather_kernel(n, *refs), in_specs=[vmem], ou...  14.1 us
    gather x7, local copies, waits for them, and re-layouts, take_rows(): return jax.vmap(lambda rows, chosen: rows[chosen])(table, wanted)  3.76 us

profile of v3, /device:TPU:0, one launch (start us, length us, event | category | flops | bytes accessed | tf_op | source)
XLA Modules:
  0.0 133.6 jit_solution(6479135762983958857)
XLA Ops:
  0.6 0.0 copy-start
  0.6 0.0 copy-start.7
  1.4 0.7 compare_and_fusion
  2.1 0.1 copy.25
  2.2 0.1 broadcast_in_dim.91
  2.3 0.7 fusion.13
  3.0 0.1 copy.26
  3.0 0.1 reshape.140
  3.1 0.7 fusion.17
  3.8 0.1 copy.27
  3.9 0.1 reshape.146
  4.0 0.7 gather_fusion.1
  4.7 0.1 iota_compare_fusion.4
  4.8 0.1 reshape.160
  4.8 0.2 slice_reduce_fusion.1
  5.0 0.1 iota_compare_fusion.2
  5.1 1.3 dynamic_slice.3
  6.4 0.3 fusion.2
  6.7 0.0 copy-start.2
  6.7 2.0 %fusion = f32[2,1024,64]{1,2,0:T(8,128)S(1)} fusion(s32[2,1024]{1,0:T(2,128)S(1)} %bitcast.84, bf16[2,1024,32]{1,2,0:T(8,128)(2,1)S(1)} %get-tuple-element.16, bf16[2,1024,32]{1,2,0:T(8,128)(2,1)S(1)} %get-tuple-element.15), kind=kOutput, calls=%fused_computation.4 | convolution fusion | flops 271056896 | bytes 794624 | tf_op jit(solution)/shard_map/bpr,brj->bpj/dot_general | solution.py:125
  8.7 0.0 copy-start.1
  8.8 1.4 %gather_fusion.2 = bf16[8,128,256]{2,1,0:T(8,128)(2,1)} fusion(bf16[4,4,128,256]{3,2,1,0:T(8,128)(2,1)S(1)} %copy-done.2, s32[8]{0:T(128)S(1)} %reshape.146), kind=kCustom, calls=%fused_computation.2 | custom fusion | bytes 1048640 | tf_op jit(solution)/shard_map/vmap()/gather | solution.py:10
  10.2 1.9 %slice_bitcast_fusion.1 = (bf16[4,128,256]{2,1,0:T(8,128)(2,1)}, bf16[4,128,256]{2,1,0:T(8,128)(2,1)}) fusion(bf16[4,2,128,256]{3,2,1,0:T(8,128)(2,1)} %bitcast.79), kind=kLoop, calls=%fused_computation.17 | loop fusion | bytes 1048576 | tf_op jit(solution)/shard_map/jit(_where)/broadcast_in_dim | solution.py:114
  12.1 1.4 %gather_fusion = bf16[8,128,256]{2,1,0:T(8,128)(2,1)} fusion(bf16[4,8,128,256]{3,2,1,0:T(8,128)(2,1)S(1)} %copy-done.1, s32[8]{0:T(128)S(1)} %reshape.140), kind=kCustom, calls=%fused_computation | custom fusion | bytes 1048640 | tf_op jit(solution)/shard_map/vmap()/gather | solution.py:10
  13.5 1.9 %broadcast_select_fusion.refs_0_ = bf16[8,128,256]{2,1,0:T(8,128)(2,1)} fusion(bf16[8,128,256]{2,1,0:T(8,128)(2,1)} %gather_fusion, pred[8]{0:T(512)(128)(4,1)S(1)} %broadcast_in_dim.91), kind=kLoop, calls=%fused_computation.8 | loop fusion | flops 262144 | bytes 1048584 | tf_op jit(solution)/shard_map/jit(_where)/select_n | solution.py:102
  15.4 14.1 %shard_map.157 = bf16[8,128,256]{2,1,0:T(8,128)(2,1)} custom-call(bf16[8,128,256]{2,1,0:T(8,128)(2,1)} %broadcast_select_fusion.refs_0_), custom_call_target="tpu_custom_call" | custom-call | tf_op jit(solution)/shard_map/pallas_call | solution.py:74
  29.5 1.1 slice_bitcast_fusion.3
  30.6 1.2 select_select_fusion.1
  31.8 1.3 copy.24
  33.1 97.2 %shard_map.158 = f32[256,1]{1,0:T(8,128)} custom-call(f32[2048,32]{1,0:T(8,128)} %bitcast.78, bf16[4,512,256]{2,1,0:T(8,128)(2,1)} %bitcast.77, bf16[1024,128]{1,0:T(8,128)(2,1)} %refs_2_.1, bf16[128,1024]{1,0:T(8,128)(2,1)} %refs_3_.1, f32[1,1024]{1,0:T(1,128)} %bitcast.83, bf16[1024,1024]{1,0:T(8,128)(2,1)} %refs_5_.1, f32[1,1024]{1,0:T(1,128)} %bitcast.85, ...), custom_call_target="tpu_custom_call" | custom-call | tf_op jit(solution)/shard_map/pallas_call | solution.py:301
  130.4 1.6 %reduce = f32[256]{0:T(256)} reduce(f32[256,1]{1,0:T(8,128)} %shard_map.158, f32[]{:T(128)} %constant.99), dimensions={1}, to_apply=%pallas_call.7.reduce_sub_computation | reduce | bytes 2052 | tf_op jit(solution)/shard_map/pallas_call | solution.py:301
  132.0 1.6 %select_select_fusion = bf16[4,8,128,256]{3,2,1,0:T(8,128)(2,1)} fusion(bf16[4,8,128,256]{3,2,1,0:T(8,128)(2,1)S(1)} %copy-done.1, pred[4,8]{1,0:T(4,128)(4,1)S(1)} %get-tuple-element.21, pred[4,8]{1,0:T(4,128)(4,1)S(1)} %get-tuple-element.22, bf16[4,128,256]{2,1,0:T(8,128)(2,1)S(1)} %copy-done.4, bf16[4,128,256]{2,1,0:T(8,128)(2,1)S(1)} %copy-done.3), kind=kLoop, calls=%fused_computation.6 | loop fusion | flops 2097152 | bytes 4718656 | tf_op jit(solution)/shard_map/jit(_where)/select_n | solution.py:114
  (17 shorter events, 0.1 us)
Async XLA Ops:
  0.6 3.4 %copy-start = (s32[4,4]{1,0:T(4,128)S(1)}, s32[4,4]{1,0:T(4,128)}, u32[]{:S(2)}) copy-start(s32[4,4]{1,0:T(4,128)} %param.16) | copy-start | bytes 196
  0.6 4.0 %copy-start.7 = (s32[4,2]{0,1:T(2,128)S(1)}, s32[4,2]{0,1:T(2,128)}, u32[]{:S(2)}) copy-start(s32[4,2]{0,1:T(2,128)} %param.18) | copy-start | bytes 100
  0.7 5.7 %copy-start.6 = (s32[2,1,1024]{2,1,0:T(1,128)S(1)}, s32[2,1,1024]{2,1,0:T(1,128)}, u32[]{:S(2)}) copy-start(s32[2,1,1024]{2,1,0:T(1,128)} %param.20) | copy-start | bytes 24580
  0.7 5.7 %copy-start.5 = (s32[2,1024,4,8]{1,3,2,0:T(8,128)S(1)}, s32[2,1024,4,8]{1,3,2,0:T(8,128)}, u32[]{:S(2)}) copy-start(s32[2,1024,4,8]{1,3,2,0:T(8,128)} %param.19) | copy-start | bytes 786436
  6.7 2.2 %copy-start.2 = (bf16[4,4,128,256]{3,2,1,0:T(8,128)(2,1)S(1)}, bf16[4,4,128,256]{3,2,1,0:T(8,128)(2,1)}, u32[]{:S(2)}) copy-start(bf16[4,4,128,256]{3,2,1,0:T(8,128)(2,1)} %param.14) | copy-start | bytes 3145732
  8.7 3.4 %copy-start.1 = (bf16[4,8,128,256]{3,2,1,0:T(8,128)(2,1)S(1)}, bf16[4,8,128,256]{3,2,1,0:T(8,128)(2,1)}, u32[]{:S(2)}) copy-start(bf16[4,8,128,256]{3,2,1,0:T(8,128)(2,1)} %param.15) | copy-start | bytes 6291460
  33.1 98.8 %copy-start.3 = (bf16[4,128,256]{2,1,0:T(8,128)(2,1)S(1)}, bf16[4,128,256]{2,1,0:T(8,128)(2,1)}, u32[]{:S(2)}) copy-start(bf16[4,128,256]{2,1,0:T(8,128)(2,1)} %get-tuple-element.11) | copy-start | bytes 786436
  33.1 98.8 %copy-start.4 = (bf16[4,128,256]{2,1,0:T(8,128)(2,1)S(1)}, bf16[4,128,256]{2,1,0:T(8,128)(2,1)}, u32[]{:S(2)}) copy-start(bf16[4,128,256]{2,1,0:T(8,128)(2,1)} %get-tuple-element.12) | copy-start | bytes 786436
